TPU v7x, 32 devices: a whole 2x2x4 slice. The times are simulated.
32 devices in a mesh: front: 2 (over core), row: 4 (over y, x), col: 4 (over z).
Axes of the slice: x: 2, y: 2, z: 4, core: 2. Of those that a mesh axis runs over, the one named last changes fastest.
Arguments:
- child_blocks: bfloat16 [16384, 8192], P(('front', 'row'), 'col'), may hold values from -0.0625 to 0.0625
- sketch: bfloat16 [8192, 512], P('col'), may hold values from -6 to 6
- block_map: int32 [2, 64], P('front'), may hold values from 0 to 95, as said below
Outputs:
- parent_basis: float32 [512, 12288], P('col', ('front', 'row'))
Inputs may be any that keep to these rules, and one draw needn't show every extreme that they name: `block_map`: each row lists 8192 / 128 different parent blocks in increasing order.
All inputs are finite; a program needn't handle non-finite values.
Results may differ from a plain program's by a relative error of at most 0.0003.
Values sent between devices are 32-bit elements; how exact they have to be, the bound alone decides.
No kernel may reach another device: no remote copies, remote signals or barrier semaphores. Data moves between devices by JAX's collectives and lax.ppermute only.
A program may use at most 128 MiB of HBM per device.

v0:
```python
import jax
import jax.numpy as jnp
from jax import lax
from jax.sharding import PartitionSpec as P

P_SIZE = 12288
BLK = 128


def from_partner(array, axis, stride):
    return lax.ppermute(array, axis, [(i, i ^ 1 << stride) for i in range(lax.axis_size(axis))])


def shards(child_blocks, sketch, block_map):
    siblings = min(4, lax.axis_size("front"))
    levels = siblings.bit_length() - 1
    front_here = lax.axis_index("front")
    row_here = lax.axis_index("row")
    row_count = lax.axis_size("row")
    sketch_part = lax.psum_scatter(
        lax.dot_general(
            sketch, child_blocks, (((0,), (1,)), ((), ())), preferred_element_type=jnp.float32
        ),
        "col",
        scatter_dimension=0,
        tiled=True,
    )
    width_here = sketch_part.shape[0]
    parent_blocks = P_SIZE // BLK
    share_blocks = parent_blocks // (siblings * row_count)
    rows_all = lax.all_gather(sketch_part, "row", axis=1, tiled=True)
    maps_all = block_map[0]
    block_count = maps_all.shape[0]
    capacity = min(share_blocks, block_count)
    blocks_all = rows_all.reshape(width_here, block_count, BLK)
    dest_share = maps_all // share_blocks
    dest_sibling = dest_share // row_count
    dest_row = dest_share % row_count
    place_plus = (maps_all % share_blocks + 1).astype(jnp.float32)
    sibling_here = front_here % siblings
    slot_ids = jnp.arange(capacity, dtype=jnp.int32)
    place_ids = jnp.arange(share_blocks, dtype=jnp.int32).astype(jnp.float32)
    share = jnp.zeros((width_here, share_blocks, BLK), jnp.float32)
    for offset_bits in range(siblings):
        target_sibling = jnp.bitwise_xor(sibling_here, offset_bits)
        wanted = (dest_sibling == target_sibling) & (dest_row == row_here)
        slot = jnp.cumsum(wanted.astype(jnp.int32)) - 1
        select = (wanted[:, None] & (slot[:, None] == slot_ids[None, :])).astype(jnp.float32)
        packed = jnp.einsum("cbk,bj->cjk", blocks_all, select, precision=lax.Precision.HIGHEST)
        places = jnp.dot(place_plus, select, precision=lax.Precision.HIGHEST) - 1.0
        for bit_level in range(levels):
            if offset_bits >> bit_level & 1:
                packed, places = from_partner((packed, places), "front", bit_level)
        landing = (places[:, None] == place_ids[None, :]).astype(jnp.float32)
        share = share + jnp.einsum("cjk,jm->cmk", packed, landing, precision=lax.Precision.HIGHEST)
    share = share.reshape(width_here, share_blocks * BLK)
    columns_all = lax.all_gather(share, "col", axis=0, tiled=True)
    gram = lax.dot_general(
        columns_all, columns_all, (((1,), (1,)), ((), ())), precision=lax.Precision.HIGHEST
    )
    gram = lax.psum(gram, "row")
    for bit_level in range(levels):
        gram = gram + from_partner(gram, "front", bit_level)
    lower = jnp.linalg.cholesky(gram)
    basis = jax.scipy.linalg.solve_triangular(lower, columns_all, lower=True)
    return lax.dynamic_slice_in_dim(basis, lax.axis_index("col") * width_here, width_here, 0)


def solution(mesh):
    placed = (P(("front", "row"), "col"), P("col", None), P("front", None))
    return jax.shard_map(
        shards, mesh=mesh, in_specs=placed, out_specs=P("col", ("front", "row")), check_vma=False
    )
```

profile of v0, /device:TPU:0, one launch (start us, length us, event | category | flops | bytes accessed | tf_op | source)
XLA Modules:
  0.0 458.2 jit_solution(8747269671987431088)
XLA Ops:
  6.5 1.6 copy-done
  8.1 9.6 %fusion.80 = f32[512,2048]{1,0:T(8,128)} fusion(bf16[2048,512]{1,0:T(8,128)(2,1)S(1)} %copy-done, bf16[2048,2048]{1,0:T(8,128)(2,1)} %param.3), kind=kOutput, calls=%fused_computation.141 | convolution fusion | flops 4294967296 | bytes 14680064 | tf_op jit(solution)/shard_map/dot_general | solution.py:21
  17.8 79.6 %reduce-scatter.2.cloned.1.call-done = f32[128,2048]{1,0:T(8,128)} async-done(((f32[512,2048]{1,0:T(8,128)}), f32[128,2048]{1,0:T(8,128)}) %reduce-scatter.2.cloned.1.call-update) | async-done | bytes 1048592 | tf_op jit(solution)/shard_map/reduce_scatter | solution.py:20
  98.4 53.9 %all-gather.3.cloned.1.call-done = f32[128,8192]{1,0:T(8,128)} async-done(((f32[128,2048]{1,0:T(8,128)}), f32[128,8192]{1,0:T(8,128)}) %all-gather.3.cloned.1.call-update) | async-done | bytes 4194320 | tf_op jit(solution)/shard_map/all_gather | solution.py:31
  152.4 2.9 copy.25
  155.3 1.5 convolution_bitcast_fusion
  157.3 1.6 convolution_bitcast_fusion.1
  158.9 0.6 fusion.51
  159.5 1.0 fusion.8
  160.6 1.2 copy.20
  161.8 2.3 copy.21
  164.3 63.5 %all-gather.5.cloned.1.call-done = f32[512,1536]{1,0:T(8,128)} async-done(((f32[128,1536]{1,0:T(8,128)}), f32[512,1536]{1,0:T(8,128)}) %all-gather.5.cloned.1.call-update) | async-done | bytes 3145744 | tf_op jit(solution)/shard_map/all_gather | solution.py:57
  227.9 9.4 %fusion.81 = f32[512,512]{0,1:T(8,128)} fusion(f32[512,1536]{1,0:T(8,128)} %all-gather.5.cloned.1.call-done), kind=kOutput, calls=%fused_computation.142 | convolution fusion | flops 4831838208 | bytes 4194304 | tf_op jit(solution)/shard_map/dot_general | solution.py:58
  237.3 51.2 %all-reduce.3.cloned.1.call-done = f32[512,512]{0,1:T(8,128)} async-done(((f32[512,512]{0,1:T(8,128)}), f32[512,512]{0,1:T(8,128)}) %all-reduce.3.cloned.1.call-update) | async-done | bytes 1048592 | tf_op jit(solution)/shard_map/psum | solution.py:61
  288.5 3.0 collective-permute-done.2
  291.5 1.7 add.150
  293.3 1.3 copy.23
  294.6 1.4 fusion.11
  296.1 1.0 copy-done.2
  297.0 11.7 %cholesky.104 = f32[128,128]{1,0:T(8,128)S(1)} custom-call(f32[128,128]{1,0:T(8,128)S(1)} %cholesky.266), custom_call_target="Cholesky" | custom-call | tf_op jit(solution)/shard_map/jit(cholesky)/cholesky | solution.py:64
  308.9 9.8 %custom-call.31 = f32[1,128,128]{1,2,0:T(8,128)S(1)} custom-call(f32[1,128,128]{2,1,0:T(8,128)S(1)} %get-tuple-element.38), custom_call_target="InvertDiagBlocksLowerTriangular" | custom-call | tf_op jit(solution)/shard_map/jit(cholesky)/cholesky | solution.py:64
  318.7 1.2 constant_dynamic-update-slice_fusion
  320.0 1.3 slice_subtract_fusion
  321.3 11.7 %cholesky.217 = f32[128,128]{1,0:T(8,128)S(1)} custom-call(f32[128,128]{1,0:T(8,128)S(1)} %cholesky.270), custom_call_target="Cholesky" | custom-call | tf_op jit(solution)/shard_map/jit(cholesky)/cholesky | solution.py:64
  333.0 10.2 %custom-call.32 = f32[1,128,128]{1,2,0:T(8,128)S(1)} custom-call(f32[1,128,128]{2,1,0:T(8,128)S(1)} %get-tuple-element.35), custom_call_target="InvertDiagBlocksLowerTriangular" | custom-call | tf_op jit(solution)/shard_map/jit(cholesky)/cholesky | solution.py:64
  343.5 1.3 slice_subtract_fusion.1
  344.8 11.7 %cholesky.238 = f32[128,128]{1,0:T(8,128)S(1)} custom-call(f32[128,128]{1,0:T(8,128)S(1)} %cholesky.275), custom_call_target="Cholesky" | custom-call | tf_op jit(solution)/shard_map/jit(cholesky)/cholesky | solution.py:64
  356.5 9.8 %custom-call.33 = f32[1,128,128]{1,2,0:T(8,128)S(1)} custom-call(f32[1,128,128]{2,1,0:T(8,128)S(1)} %get-tuple-element.32), custom_call_target="InvertDiagBlocksLowerTriangular" | custom-call | tf_op jit(solution)/shard_map/jit(cholesky)/cholesky | solution.py:64
  366.5 1.2 slice_subtract_fusion.2
  367.8 11.9 %cholesky.255 = f32[128,128]{1,0:T(8,128)S(1)} custom-call(f32[128,128]{1,0:T(8,128)S(1)} %slice_subtract_fusion.2), custom_call_target="Cholesky" | custom-call | tf_op jit(solution)/shard_map/jit(cholesky)/cholesky | solution.py:64
  379.7 0.6 compare_reduce_fusion.1
  380.3 0.6 compare_reduce_fusion
  380.9 0.7 compare_reduce_fusion.2
  384.1 1.1 select_select_fusion
  385.2 13.8 %while.1 = (s32[]{:T(128)}, f32[512,512]{1,0:T(8,128)}, s32[4,2]{0,1:T(2,128)S(1)}, f32[4,128,128]{2,1,0:T(8,128)}, s32[]{:T(128)}) while((s32[]{:T(128)}, f32[512,512]{1,0:T(8,128)}, s32[4,2]{0,1:T(2,128)S(1)}, f32[4,128,128]{2,1,0:T(8,128)}, s32[]{:T(128)}) %tuple.31), condition=%wide.while_cond, body=%wide.while_body.sunk | while | flops 2 | bytes 132205 | solution.py:65
  385.8 2.9 bitcast_dynamic-update-slice_fusion.2
  389.3 2.9 bitcast_dynamic-update-slice_fusion.2
  392.7 2.9 bitcast_dynamic-update-slice_fusion.2
  396.2 2.8 bitcast_dynamic-update-slice_fusion.2
  399.0 40.1 %custom-call.34 = f32[4,128,128]{1,2,0:T(8,128)S(1)} custom-call(f32[4,128,128]{2,1,0:T(8,128)} %get-tuple-element.12), custom_call_target="InvertDiagBlocksLowerTriangular" | custom-call | tf_op jit(solution)/shard_map/jit(_solve_triangular)/triangular_solve | solution.py:65
  439.1 2.1 fusion.16
  441.3 2.0 convolution_subtract_fusion.2
  443.2 0.8 fusion.31
  444.1 1.9 convolution_subtract_fusion
  446.0 0.8 fusion.29
  446.9 2.5 convolution_subtract_fusion.1
  449.4 0.8 fusion.28
  450.2 1.3 fusion.15
  (55 shorter events, 5.0 us)
Async XLA Ops:
  6.5 1.6 copy-start
  6.5 90.9 %reduce-scatter.2.cloned.1.call-start = ((), (), s32[]{:S(2)}) async-start(), calls=%async_computation.1 | async-start | bytes 5242880 | tf_op jit(solution)/shard_map/reduce_scatter | solution.py:20
  17.7 79.8 %copy-start.3 = (s32[1,64]{1,0:T(1,128)S(1)}, s32[1,64]{1,0:T(1,128)}, u32[]{:S(2)}) copy-start(s32[1,64]{1,0:T(1,128)} %param.5) | copy-start | bytes 772
  17.7 134.6 %all-gather.3.cloned.1.call-start = ((), (), s32[]{:S(2)}) async-start(), calls=%async_computation.2 | async-start | bytes 5242880 | tf_op jit(solution)/shard_map/all_gather | solution.py:31
  97.4 130.4 %all-gather.5.cloned.1.call-start = ((), (), s32[]{:S(2)}) async-start(), calls=%async_computation.3 | async-start | bytes 3932160 | tf_op jit(solution)/shard_map/all_gather | solution.py:57
  98.2 61.3 %collective-permute-start = (f32[12]{0:T(128)S(1)}, f32[12]{0:T(128)S(1)}, u32[]{:S(2)}, u32[]{:S(2)}) collective-permute-start(f32[12]{0:T(128)S(1)} %fusion.9), channel_id=1, source_target_pairs={{0,16},{16,0},{1,17},{17,1},{2,18},{18,2},{3,19},{19,3},{4,20},{20... | collective-permute-start | bytes 152 | tf_op jit(solution)/shard_map/ppermute | solution.py:11
  157.1 2.4 collective-permute-start.1
  164.1 124.4 %all-reduce.3.cloned.1.call-start = ((), (), s32[]{:S(2)}) async-start(), calls=%async_computation.4 | async-start | bytes 2097152 | tf_op jit(solution)/shard_map/psum | solution.py:61
  288.5 3.0 collective-permute-start.2
  296.1 1.0 copy-start.2
  439.1 5.0 %copy-start.1 = (f32[512,1536]{1,0:T(8,128)S(1)}, f32[512,1536]{1,0:T(8,128)}, u32[]{:S(2)}) copy-start(f32[512,1536]{1,0:T(8,128)} %all-gather.5.cloned.1.call-done) | copy-start | bytes 9437188
Sparse Core Ops, SparseCore 0:
  17.9 79.5 reduce-scatter.1
  99.3 53.0 all-gather.2
  164.2 63.5 all-gather.4
  237.4 51.0 all-reduce.2
where the time goes:
time: 466 us; the launch traced here: 458 us
  waiting for transfers between devices  251 us (54%)
  other arithmetic  125 us (27%)
  matrix products  40.5 us (9%)
  local copies, waits for them, and re-layouts  24.8 us (5%)
  between operations  16.1 us (3%)
    reduce_scatter x1, waiting for transfers between devices, shards(): lax.psum_scatter(lax.dot_general(sketch, child_blocks, (((0,), (1,)), (()...  79.6 us
    another operation x14, other arithmetic, shards(): lower = jnp.linalg.cholesky(gram)  78.9 us
    all_gather x1, waiting for transfers between devices, shards(): columns_all = lax.all_gather(share, 'col', axis=0, tiled=True)  63.5 us
    all_gather x1, waiting for transfers between devices, shards(): rows_all = lax.all_gather(sketch_part, 'row', axis=1, tiled=True)  53.9 us
    psum x1, waiting for transfers between devices, shards(): gram = lax.psum(gram, 'row')  51.2 us
    another operation x4, other arithmetic, shards(): basis = jax.scipy.linalg.solve_triangular(lower, columns_all, lower=True)  42.5 us
    another operation x12, local copies, waits for them, and re-layouts  13.8 us
    another operation x7, matrix products, shards(): basis = jax.scipy.linalg.solve_triangular(lower, columns_all, lower=True)  11 us
  transfers between devices with their start and end apart: 7, of which 5 were waited for; matrix products, arithmetic and copies ran while one was open for 2% of the time, Pallas kernels for 0%

commit v1 on v0

--- a/solution.py
+++ b/solution.py
@@ -5,6 +5,28 @@
 
 P_SIZE = 12288
 BLK = 128
+
+
+def joined_along(blocks, dim):
+    shape = list(blocks.shape[1:])
+    shape[dim] *= blocks.shape[0]
+    return jnp.moveaxis(blocks, 0, dim).reshape(shape)
+
+
+def gather_around(shard, axis, dim):
+    size = lax.axis_size(axis)
+    pairs = [(i, (i + 1) % size) for i in range(size)]
+    back = [(b, a) for a, b in pairs]
+    lower, upper = ([], [])
+    for step in range(size - 1):
+        if step % 2 == 0:
+            lower.append(lax.ppermute(lower[-1] if lower else shard, axis, pairs))
+        else:
+            upper.append(lax.ppermute(upper[-1] if upper else shard, axis, back))
+    parts = jnp.stack([*lower[::-1], shard, *upper])
+    shift = lax.axis_index(axis) - len(lower)
+    parts = parts[(jnp.arange(size) - shift) % size]
+    return joined_along(parts, dim)
 
 
 def from_partner(array, axis, stride):
@@ -28,7 +50,7 @@
     width_here = sketch_part.shape[0]
     parent_blocks = P_SIZE // BLK
     share_blocks = parent_blocks // (siblings * row_count)
-    rows_all = lax.all_gather(sketch_part, "row", axis=1, tiled=True)
+    rows_all = gather_around(sketch_part, "row", 1)
     maps_all = block_map[0]
     block_count = maps_all.shape[0]
     capacity = min(share_blocks, block_count)

time: 466 us -> 502 us (1.077)
  waiting for transfers between devices: 251 us -> 264 us
  local copies, waits for them, and re-layouts: 24.8 us -> 37.6 us
    ppermute x0 -> x3, waiting for transfers between devices: none -> 66.3 us  [the longest x2 44.8 us: gather_around(): lower.append(lax.ppermute(lower[-1] if lower else shard, axis, pairs))]
    all_gather x1 -> x0, waiting for transfers between devices: 53.9 us -> none  [shards(): rows_all = lax.all_gather(sketch_part, 'row', axis=1, tiled=True)]
    another operation x12 -> x13, local copies, waits for them, and re-layouts: 13.8 us -> 19.2 us
    transpose x0 -> x1, local copies, waits for them, and re-layouts: none -> 5.34 us  [joined_along(): return jnp.moveaxis(blocks, 0, dim).reshape(shape)]
  transfers between devices with their start and end apart: 7 -> 9, of which waited for: 5 -> 7; matrix products, arithmetic and copies ran while one was open for 2% -> 6% of each run, Pallas kernels for 0% -> 0%
where the time goes in v1:
time: 502 us; the launch traced here: 493 us
  waiting for transfers between devices  264 us (53%)
  other arithmetic  129 us (26%)
  matrix products  42.7 us (9%)
  local copies, waits for them, and re-layouts  37.6 us (7%)
  between operations  16 us (3%)
    reduce_scatter x1, waiting for transfers between devices, shards(): lax.psum_scatter(lax.dot_general(sketch, child_blocks, (((0,), (1,)), (()...  79.6 us
    another operation x14, other arithmetic, shards(): lower = jnp.linalg.cholesky(gram)  78.9 us
    all_gather x1, waiting for transfers between devices, shards(): columns_all = lax.all_gather(share, 'col', axis=0, tiled=True)  63.4 us
    psum x1, waiting for transfers between devices, shards(): gram = lax.psum(gram, 'row')  51.3 us
    ppermute x2, waiting for transfers between devices, gather_around(): lower.append(lax.ppermute(lower[-1] if lower else shard, axis, pairs))  44.8 us
    another operation x4, other arithmetic, shards(): basis = jax.scipy.linalg.solve_triangular(lower, columns_all, lower=True)  42.5 us
    ppermute x1, waiting for transfers between devices, gather_around(): upper.append(lax.ppermute(upper[-1] if upper else shard, axis, back))  21.5 us
    another operation x12, local copies, waits for them, and re-layouts  13.8 us
  transfers between devices with their start and end apart: 9, of which 7 were waited for; matrix products, arithmetic and copies ran while one was open for 6% of the time, Pallas kernels for 0%

profile of v1, /device:TPU:0, one launch (start us, length us, event | category | flops | bytes accessed | tf_op | source)
XLA Modules:
  0.0 493.2 jit_solution(11993610545763506369)
XLA Ops:
  6.5 1.6 copy-done
  8.1 9.6 %fusion.82 = f32[512,2048]{1,0:T(8,128)} fusion(bf16[2048,512]{1,0:T(8,128)(2,1)S(1)} %copy-done, bf16[2048,2048]{1,0:T(8,128)(2,1)} %param.3), kind=kOutput, calls=%fused_computation.150 | convolution fusion | flops 4294967296 | bytes 14680064 | tf_op jit(solution)/shard_map/dot_general | solution.py:43
  17.8 79.6 %reduce-scatter.2.cloned.1.call-done = f32[128,2048]{1,0:T(8,128)} async-done(((f32[512,2048]{1,0:T(8,128)}), f32[128,2048]{1,0:T(8,128)}) %reduce-scatter.2.cloned.1.call-update) | async-done | bytes 1048592 | tf_op jit(solution)/shard_map/reduce_scatter | solution.py:42
  97.4 1.5 collective-permute-start
  99.3 1.5 collective-permute-start.2
  100.8 23.8 %collective-permute-done = f32[128,2048]{1,0:T(8,128)S(1)} collective-permute-done((f32[128,2048]{1,0:T(8,128)}, f32[128,2048]{1,0:T(8,128)S(1)}, u32[]{:S(2)}, u32[]{:S(2)}) %collective-permute-start) | collective-permute-done | bytes 1048608 | tf_op jit(solution)/shard_map/ppermute | solution.py:23
  125.7 21.5 %collective-permute-done.2 = f32[128,2048]{1,0:T(8,128)} collective-permute-done((f32[128,2048]{1,0:T(8,128)}, f32[128,2048]{1,0:T(8,128)}, u32[]{:S(2)}, u32[]{:S(2)}) %collective-permute-start.2) | collective-permute-done | bytes 1048608 | tf_op jit(solution)/shard_map/ppermute | solution.py:25
  147.2 21.0 %collective-permute-done.1 = f32[128,2048]{1,0:T(8,128)} collective-permute-done((f32[128,2048]{1,0:T(8,128)S(1)}, f32[128,2048]{1,0:T(8,128)}, u32[]{:S(2)}, u32[]{:S(2)}) %collective-permute-start.1) | collective-permute-done | bytes 1048608 | tf_op jit(solution)/shard_map/ppermute | solution.py:23
  168.2 4.2 pad_maximum_fusion
  172.4 5.0 %gather_fusion = f32[4,128,2048]{2,1,0:T(8,128)} fusion(f32[4,128,2048]{2,1,0:T(8,128)} %pad_maximum_fusion, s32[1024]{0:T(1024)S(1)} %pad_clamp_fusion), kind=kCustom, calls=%fused_computation | custom fusion | bytes 8388624 | tf_op jit(solution)/shard_map/gather | solution.py:28
  177.3 5.3 %copy.19 = f32[128,4,2048]{0,2,1:T(8,128)} copy(f32[128,4,2048]{2,0,1:T(8,128)} %bitcast.112) | data formatting | bytes 8388608 | tf_op jit(solution)/shard_map/transpose | solution.py:13
  182.7 5.4 %copy.20 = f32[128,64,128]{2,1,0:T(8,128)} copy(f32[128,64,128]{0,2,1:T(8,128)} %bitcast.113) | data formatting | bytes 8388608 | tf_op jit(solution)/shard_map/reshape;reshape | solution.py:57
  188.1 3.8 convolution_bitcast_fusion
  192.4 1.6 convolution_bitcast_fusion.1
  194.6 1.0 fusion.8
  195.6 1.2 copy.24
  196.9 2.3 copy.25
  199.4 63.4 %all-gather.2.cloned.1.call-done = f32[512,1536]{1,0:T(8,128)} async-done(((f32[128,1536]{1,0:T(8,128)}), f32[512,1536]{1,0:T(8,128)}) %all-gather.2.cloned.1.call-update) | async-done | bytes 3145744 | tf_op jit(solution)/shard_map/all_gather | solution.py:79
  262.8 9.4 %fusion.83 = f32[512,512]{0,1:T(8,128)} fusion(f32[512,1536]{1,0:T(8,128)} %all-gather.2.cloned.1.call-done), kind=kOutput, calls=%fused_computation.151 | convolution fusion | flops 4831838208 | bytes 4194304 | tf_op jit(solution)/shard_map/dot_general | solution.py:80
  272.2 51.3 %all-reduce.3.cloned.1.call-done = f32[512,512]{0,1:T(8,128)} async-done(((f32[512,512]{0,1:T(8,128)}), f32[512,512]{0,1:T(8,128)}) %all-reduce.3.cloned.1.call-update) | async-done | bytes 1048592 | tf_op jit(solution)/shard_map/psum | solution.py:83
  323.5 3.0 collective-permute-done.5
  326.5 1.7 add.176
  328.2 1.3 copy.27
  329.6 1.4 fusion.11
  331.0 1.0 copy-done.3
  332.0 11.7 %cholesky.104 = f32[128,128]{1,0:T(8,128)S(1)} custom-call(f32[128,128]{1,0:T(8,128)S(1)} %cholesky.266), custom_call_target="Cholesky" | custom-call | tf_op jit(solution)/shard_map/jit(cholesky)/cholesky | solution.py:86
  343.9 9.8 %custom-call.31 = f32[1,128,128]{1,2,0:T(8,128)S(1)} custom-call(f32[1,128,128]{2,1,0:T(8,128)S(1)} %get-tuple-element.38), custom_call_target="InvertDiagBlocksLowerTriangular" | custom-call | tf_op jit(solution)/shard_map/jit(cholesky)/cholesky | solution.py:86
  353.7 1.2 constant_dynamic-update-slice_fusion
  354.9 1.3 slice_subtract_fusion
  356.2 11.7 %cholesky.217 = f32[128,128]{1,0:T(8,128)S(1)} custom-call(f32[128,128]{1,0:T(8,128)S(1)} %cholesky.270), custom_call_target="Cholesky" | custom-call | tf_op jit(solution)/shard_map/jit(cholesky)/cholesky | solution.py:86
  368.0 10.2 %custom-call.32 = f32[1,128,128]{1,2,0:T(8,128)S(1)} custom-call(f32[1,128,128]{2,1,0:T(8,128)S(1)} %get-tuple-element.35), custom_call_target="InvertDiagBlocksLowerTriangular" | custom-call | tf_op jit(solution)/shard_map/jit(cholesky)/cholesky | solution.py:86
  378.4 1.3 slice_subtract_fusion.1
  379.7 11.7 %cholesky.238 = f32[128,128]{1,0:T(8,128)S(1)} custom-call(f32[128,128]{1,0:T(8,128)S(1)} %cholesky.275), custom_call_target="Cholesky" | custom-call | tf_op jit(solution)/shard_map/jit(cholesky)/cholesky | solution.py:86
  391.5 9.8 %custom-call.33 = f32[1,128,128]{1,2,0:T(8,128)S(1)} custom-call(f32[1,128,128]{2,1,0:T(8,128)S(1)} %get-tuple-element.32), custom_call_target="InvertDiagBlocksLowerTriangular" | custom-call | tf_op jit(solution)/shard_map/jit(cholesky)/cholesky | solution.py:86
  401.5 1.2 slice_subtract_fusion.2
  402.7 11.9 %cholesky.255 = f32[128,128]{1,0:T(8,128)S(1)} custom-call(f32[128,128]{1,0:T(8,128)S(1)} %slice_subtract_fusion.2), custom_call_target="Cholesky" | custom-call | tf_op jit(solution)/shard_map/jit(cholesky)/cholesky | solution.py:86
  419.0 1.1 select_select_fusion
  420.1 13.8 %while.1 = (s32[]{:T(128)}, f32[512,512]{1,0:T(8,128)}, s32[4,2]{0,1:T(2,128)S(1)}, f32[4,128,128]{2,1,0:T(8,128)}, s32[]{:T(128)}) while((s32[]{:T(128)}, f32[512,512]{1,0:T(8,128)}, s32[4,2]{0,1:T(2,128)S(1)}, f32[4,128,128]{2,1,0:T(8,128)}, s32[]{:T(128)}) %tuple.31), condition=%wide.while_cond, body=%wide.while_body.sunk | while | flops 2 | bytes 132205 | solution.py:87
  420.7 2.9 bitcast_dynamic-update-slice_fusion.2
  424.2 2.9 bitcast_dynamic-update-slice_fusion.2
  427.7 2.9 bitcast_dynamic-update-slice_fusion.2
  431.2 2.8 bitcast_dynamic-update-slice_fusion.2
  434.0 40.1 %custom-call.34 = f32[4,128,128]{1,2,0:T(8,128)S(1)} custom-call(f32[4,128,128]{2,1,0:T(8,128)} %get-tuple-element.12), custom_call_target="InvertDiagBlocksLowerTriangular" | custom-call | tf_op jit(solution)/shard_map/jit(_solve_triangular)/triangular_solve | solution.py:87
  474.1 2.1 fusion.16
  476.2 2.0 convolution_subtract_fusion.2
  479.0 1.9 convolution_subtract_fusion
  481.8 2.5 convolution_subtract_fusion.1
  485.2 1.3 fusion.15
  (65 shorter events, 10.6 us)
Async XLA Ops:
  6.5 1.6 copy-start
  6.5 90.9 %reduce-scatter.2.cloned.1.call-start = ((), (), s32[]{:S(2)}) async-start(), calls=%async_computation.1 | async-start | bytes 5242880 | tf_op jit(solution)/shard_map/reduce_scatter | solution.py:42
  17.7 81.2 %copy-start.4 = (s32[1,64]{1,0:T(1,128)S(1)}, s32[1,64]{1,0:T(1,128)}, u32[]{:S(2)}) copy-start(s32[1,64]{1,0:T(1,128)} %param.5) | copy-start | bytes 772
  17.7 245.0 %all-gather.2.cloned.1.call-start = ((), (), s32[]{:S(2)}) async-start(), calls=%async_computation.2 | async-start | bytes 3932160 | tf_op jit(solution)/shard_map/all_gather | solution.py:79
  97.4 27.1 %collective-permute-start = (f32[128,2048]{1,0:T(8,128)}, f32[128,2048]{1,0:T(8,128)S(1)}, u32[]{:S(2)}, u32[]{:S(2)}) collective-permute-start(f32[128,2048]{1,0:T(8,128)} %reduce-scatter.2.cloned.1.call-done), channel_id=1, source_target_pairs={{0,4},{4,8},{8,12},{12,0},{1,5},{5,9},{9,13},{13,1},{2,6},{6,10},{... | collective-permute-start | bytes 3145736 | tf_op jit(solution)/shard_map/ppermute | solution.py:23
  99.3 47.9 %collective-permute-start.2 = (f32[128,2048]{1,0:T(8,128)}, f32[128,2048]{1,0:T(8,128)}, u32[]{:S(2)}, u32[]{:S(2)}) collective-permute-start(f32[128,2048]{1,0:T(8,128)} %reduce-scatter.2.cloned.1.call-done), channel_id=1, source_target_pairs={{4,0},{8,4},{12,8},{0,12},{5,1},{9,5},{13,9},{1,13},{6,2},{10,6},{... | collective-permute-start | bytes 3145736 | tf_op jit(solution)/shard_map/ppermute | solution.py:25
  124.6 43.6 %collective-permute-start.1 = (f32[128,2048]{1,0:T(8,128)S(1)}, f32[128,2048]{1,0:T(8,128)}, u32[]{:S(2)}, u32[]{:S(2)}) collective-permute-start(f32[128,2048]{1,0:T(8,128)S(1)} %collective-permute-done), channel_id=1, source_target_pairs={{0,4},{4,8},{8,12},{12,0},{1,5},{5,9},{9,13},{13,1},{2,6},{6,10},{... | collective-permute-start | bytes 3145736 | tf_op jit(solution)/shard_map/ppermute | solution.py:23
  125.4 69.2 %collective-permute-start.3 = (f32[12]{0:T(128)S(1)}, f32[12]{0:T(128)S(1)}, u32[]{:S(2)}, u32[]{:S(2)}) collective-permute-start(f32[12]{0:T(128)S(1)} %fusion.9), channel_id=1, source_target_pairs={{0,16},{16,0},{1,17},{17,1},{2,18},{18,2},{3,19},{19,3},{4,20},{20... | collective-permute-start | bytes 152 | tf_op jit(solution)/shard_map/ppermute | solution.py:33
  188.1 4.3 copy-start.1
  192.2 2.4 collective-permute-start.4
  199.2 124.3 %all-reduce.3.cloned.1.call-start = ((), (), s32[]{:S(2)}) async-start(), calls=%async_computation.3 | async-start | bytes 2097152 | tf_op jit(solution)/shard_map/psum | solution.py:83
  323.5 3.0 collective-permute-start.5
  331.0 1.0 copy-start.3
  474.1 5.0 %copy-start.2 = (f32[512,1536]{1,0:T(8,128)S(1)}, f32[512,1536]{1,0:T(8,128)}, u32[]{:S(2)}) copy-start(f32[512,1536]{1,0:T(8,128)} %all-gather.2.cloned.1.call-done) | copy-start | bytes 9437188
Sparse Core Ops, SparseCore 0:
  17.9 79.5 reduce-scatter.1
  199.3 63.4 all-gather.1
  272.3 51.0 all-reduce.2
